TPU v7x, 32 devices: a whole 2x2x4 slice. The times are simulated.
32 devices in a mesh: pairs: 8 (over y, x, core), fit: 4 (over z).
Axes of the slice: x: 2, y: 2, z: 4, core: 2. Of those that a mesh axis runs over, the one named last changes fastest.
Arguments:
- b_first: bfloat16 [64, 160, 3072], P('pairs', None, 'fit'), may hold values from -0.109375 to 0.109375
- b_second: bfloat16 [64, 160, 3072], P('pairs', None, 'fit'), may hold values from -6 to 6
- start_amplitudes: float32 [64, 160, 160], P('pairs'), may hold values from -1.8 to 1.8
- margins: bfloat16 [64, 96, 160, 160], P('pairs', 'fit'), may hold values from -0.5 to 0.5
- fock_terms: float32 [64, 96], P('pairs', 'fit'), may hold values from -0.2 to 0.2
- partners: int32 [64, 96], P('pairs', 'fit'), may hold values from 0 to 63, as said below
- pno_energy: float32 [64, 160], P('pairs'), may hold values from 0.3 to 1.5
- occ_energy: float32 [4000], replicated, may hold values from -1 to -0.2
- pair_list: int32 [64, 2], P('pairs'), may hold values from 0 to 3999
- pno_count: int32 [64], P('pairs'), may hold values from 64 to 160, as said below
Outputs:
- amplitudes: float32 [64, 160, 160], P('pairs')
- residual: float32 [64, 160, 160], P('pairs')
Inputs may be any that keep to these rules, and one draw needn't show every extreme that they name: `pno_count`: each pair's PNO count is one of 64, 128 and 160. `partners`: pairs owner * 8 to owner * 8 + 7 belong to one owner. In the block of one device (its 8 rows and the columns of its index along fit), each owner's pairs appear at most 48 times, and one owner's pairs appear exactly 48 times in every block.
All inputs are finite; a program needn't handle non-finite values.
Results may differ from a plain program's by a relative error of at most 0.0041.
Values may be sent and summed in bfloat16 or wider, within the bound.
A program may use at most 192 MiB of HBM per device.

v0:
```python
import jax
import jax.numpy as jnp
from jax import lax
from jax.sharding import PartitionSpec as P

ITERS = 2


def shards(
    b_first,
    b_second,
    start_amplitudes,
    margins,
    fock_terms,
    partners,
    pno_energy,
    occ_energy,
    pair_list,
    pno_count,
):
    pair_dev = start_amplitudes.shape[0]
    pno_width = pno_energy.shape[1]
    per_pair = partners.shape[1]
    request_count = pair_dev * per_pair
    levels = lax.broadcasted_iota(jnp.int32, (pair_dev, pno_width), 1)
    keep_rows = (levels < pno_count[:, None]).astype(jnp.float32)
    pair_mask = keep_rows[:, :, None] * keep_rows[:, None, :]
    occ_pair = occ_energy[pair_list[:, 0]] + occ_energy[pair_list[:, 1]]
    denominator = pno_energy[:, :, None] + pno_energy[:, None, :] - occ_pair[:, None, None]
    integral_part = jnp.einsum(
        "rap,rbp->rab", b_first, b_second, preferred_element_type=jnp.float32
    )
    flat_partners = partners.reshape(request_count)
    amplitudes = pair_mask * start_amplitudes
    residual = jnp.zeros_like(amplitudes)
    for iteration in range(ITERS):
        rounded = amplitudes.astype(jnp.bfloat16)
        everything = lax.all_gather(rounded, "pairs", axis=0, tiled=True)
        fetched = everything[flat_partners]
        fetched = fetched.reshape(pair_dev, per_pair, pno_width, pno_width)
        left_product = jnp.einsum(
            "rpac,rpcd->rpad", margins, fetched, preferred_element_type=jnp.float32
        ).astype(jnp.bfloat16)
        right_product = jnp.einsum(
            "rpad,rpbd->rpab", left_product, margins, preferred_element_type=jnp.float32
        )
        coupling = jnp.sum(fock_terms[:, :, None, None] * right_product, axis=1)
        partial_sum = integral_part - coupling
        reduced = lax.psum(partial_sum, "fit")
        residual = pair_mask * (reduced + denominator * amplitudes)
        amplitudes = amplitudes - residual / denominator
    return (amplitudes, residual)


def solution(mesh):
    return jax.shard_map(
        shards,
        mesh=mesh,
        in_specs=(
            P("pairs", None, "fit"),
            P("pairs", None, "fit"),
            P("pairs", None, None),
            P("pairs", "fit", None, None),
            P("pairs", "fit"),
            P("pairs", "fit"),
            P("pairs", None),
            P(),
            P("pairs", None),
            P("pairs"),
        ),
        out_specs=(P("pairs", None, None), P("pairs", None, None)),
        check_vma=False,
    )
```

profile of v0, /device:TPU:0, one launch (start us, length us, event | category | flops | bytes accessed | tf_op | source)
XLA Modules:
  0.0 302.1 jit_solution(12965872413875389841)
XLA Ops:
  7.2 0.0 copy-start
  7.2 0.0 copy-start.6
  7.2 0.0 all-gather.3.cloned.1.call-start
  7.2 0.9 fusion.15
  8.1 2.4 fusion.14
  10.5 0.0 all-gather.3.cloned.1.call-update
  10.5 0.0 all-reduce.3.cloned.1.call-start
  10.6 0.0 copy-done.6
  10.6 0.1 reshape.83
  10.7 0.0 copy-start.8
  10.7 43.7 %all-gather.3.cloned.1.call-done = bf16[64,160,160]{2,1,0:T(8,128)(2,1)} async-done(((bf16[8,160,160]{2,1,0:T(8,128)(2,1)}), bf16[64,160,160]{2,1,0:T(8,128)(2,1)}) %all-gather.3.cloned.1.call-update) | async-done | bytes 3276816 | tf_op jit(solution)/shard_map/all_gather | solution.py:38
  54.4 11.9 %gather_fusion = bf16[192,160,160]{2,1,0:T(8,128)(2,1)} fusion(bf16[64,160,160]{2,1,0:T(8,128)(2,1)} %all-gather.3.cloned.1.call-done, s32[1024]{0:T(1024)S(1)} %pad_clamp_fusion.2), kind=kCustom, calls=%fused_computation | custom fusion | bytes 19661568 | tf_op jit(solution)/shard_map/gather | solution.py:39
  66.2 0.0 copy-done.8
  66.3 21.3 %multiply_reduce_fusion.1 = f32[8,160,160]{2,1,0:T(8,128)S(1)} fusion(f32[8,24]{1,0:T(8,128)S(1)} %copy-done.8, bf16[8,24,160,160]{3,2,1,0:T(8,128)(2,1)} %param.13, bf16[8,24,160,160]{3,2,1,0:T(8,128)(2,1)} %bitcast.16), kind=kOutput, calls=%fused_computation.5 | convolution fusion | flops 3160268800 | bytes 20480768 | tf_op jit(solution)/shard_map/rpad,rpbd->rpab/dot_general | solution.py:44
  87.5 0.0 copy-done
  87.5 0.0 copy-start.7
  87.6 0.0 copy-start.2
  87.6 3.7 %fusion.20 = (f32[8,160,160]{2,1,0:T(8,128)}, f32[8,160,160]{2,1,0:T(8,128)}) fusion(f32[8,160,160]{2,1,0:T(8,128)S(1)} %multiply_reduce_fusion.1, bf16[8,160,768]{2,1,0:T(8,128)(2,1)S(1)} %copy-done, bf16[8,160,768]{2,1,0:T(8,128)(2,1)} %param.11), kind=kOutput, calls=%fused_computation.31 | convolution fusion | flops 314777600 | bytes 6389760 | tf_op jit(solution)/shard_map/rap,rbp->rab/dot_general | solution.py:30
  91.3 0.0 copy-start.3
  91.3 0.0 copy-start.5
  91.3 0.0 all-reduce.3.cloned.1.call-update
  91.3 0.0 all-gather.5.cloned.1.call-start
  91.4 0.0 copy-done.7
  91.4 0.0 copy-done.2
  91.4 0.6 gather_fusion.2
  92.1 0.6 gather_fusion.1
  92.7 58.9 %all-reduce.3.cloned.1.call-done = f32[8,160,160]{2,1,0:T(8,128)} async-done(((f32[8,160,160]{2,1,0:T(8,128)}), f32[8,160,160]{2,1,0:T(8,128)}) %all-reduce.3.cloned.1.call-update) | async-done | bytes 819216 | tf_op jit(solution)/shard_map/psum | solution.py:49
  151.6 0.0 copy-done.3
  151.6 0.0 copy-done.5
  151.6 2.7 fusion.18
  154.3 0.0 all-gather.5.cloned.1.call-update
  154.3 0.2 all-reduce.5.cloned.1.call-start
  154.5 40.5 %all-gather.5.cloned.1.call-done = bf16[64,160,160]{2,1,0:T(8,128)(2,1)} async-done(((bf16[8,160,160]{2,1,0:T(8,128)(2,1)}), bf16[64,160,160]{2,1,0:T(8,128)(2,1)}) %all-gather.5.cloned.1.call-update) | async-done | bytes 3276816 | tf_op jit(solution)/shard_map/all_gather | solution.py:38
  195.0 11.9 %gather_fusion.3 = bf16[192,160,160]{2,1,0:T(8,128)(2,1)} fusion(bf16[64,160,160]{2,1,0:T(8,128)(2,1)} %all-gather.5.cloned.1.call-done, s32[1024]{0:T(1024)S(1)} %pad_clamp_fusion.2), kind=kCustom, calls=%fused_computation.3 | custom fusion | bytes 19661568 | tf_op jit(solution)/shard_map/gather | solution.py:39
  206.9 0.0 copy-start.4
  206.9 22.4 %multiply_reduce_fusion = f32[8,160,160]{2,1,0:T(8,128)} fusion(f32[8,24]{1,0:T(8,128)S(1)} %copy-done.8, bf16[8,24,160,160]{3,2,1,0:T(8,128)(2,1)} %param.13, bf16[8,24,160,160]{3,2,1,0:T(8,128)(2,1)} %bitcast.15), kind=kOutput, calls=%fused_computation.4 | convolution fusion | flops 3160268800 | bytes 20480768 | tf_op jit(solution)/shard_map/rpad,rpbd->rpab/dot_general | solution.py:44
  229.3 0.0 copy-done.4
  229.3 2.5 sub.24
  231.8 0.0 all-reduce.5.cloned.1.call-update
  231.9 60.3 %all-reduce.5.cloned.1.call-done = f32[8,160,160]{2,1,0:T(8,128)} async-done(((f32[8,160,160]{2,1,0:T(8,128)}), f32[8,160,160]{2,1,0:T(8,128)}) %all-reduce.5.cloned.1.call-update) | async-done | bytes 819216 | tf_op jit(solution)/shard_map/psum | solution.py:49
  292.1 0.0 copy-start.1
  292.1 3.4 %divide_subtract_fusion = (f32[8,160,160]{2,1,0:T(8,128)}, f32[8,160,160]{2,1,0:T(8,128)}) fusion(f32[8,160,160]{2,1,0:T(8,128)S(1)} %get-tuple-element.5, f32[8]{0:T(128)S(1)} %add.55, f32[8,160]{1,0:T(8,128)S(1)} %copy-done.5, f32[8,160,160]{2,1,0:T(8,128)} %all-reduce.5.cloned.1.call-done, f32[8,160]{1,0:T(8,128)S(1)} %fusion.15), kind=kLoop, calls=%fused_computation.17 | loop fusion | flops 1638400 | bytes 3287072 | tf_op jit(solution)/shard_map/sub | solution.py:51
  295.5 0.0 copy-done.1
  (5 shorter events, 0.0 us)
Async XLA Ops:
  7.2 80.4 %copy-start = (bf16[8,160,768]{2,1,0:T(8,128)(2,1)S(1)}, bf16[8,160,768]{2,1,0:T(8,128)(2,1)}, u32[]{:S(2)}) copy-start(bf16[8,160,768]{2,1,0:T(8,128)(2,1)} %param.10) | copy-start | bytes 5898244
  7.2 3.4 %copy-start.6 = (s32[8,24]{1,0:T(8,128)S(1)}, s32[8,24]{1,0:T(8,128)}, u32[]{:S(2)}) copy-start(s32[8,24]{1,0:T(8,128)} %param.15) | copy-start | bytes 2308
  7.2 47.2 %all-gather.3.cloned.1.call-start = ((), (), s32[]{:S(2)}) async-start(), calls=%async_computation | async-start | bytes 5898240 | tf_op jit(solution)/shard_map/all_gather | solution.py:38
  10.5 141.1 %all-reduce.3.cloned.1.call-start = ((), (), s32[]{:S(2)}) async-start(), calls=%async_computation.1 | async-start | bytes 2621440 | tf_op jit(solution)/shard_map/psum | solution.py:49
  10.7 55.6 %copy-start.8 = (f32[8,24]{1,0:T(8,128)S(1)}, f32[8,24]{1,0:T(8,128)}, u32[]{:S(2)}) copy-start(f32[8,24]{1,0:T(8,128)} %param.14) | copy-start | bytes 2308
  87.5 3.8 %copy-start.7 = (s32[8,2]{0,1:T(2,128)S(1)}, s32[8,2]{0,1:T(2,128)}, u32[]{:S(2)}) copy-start(s32[8,2]{0,1:T(2,128)} %param.18) | copy-start | bytes 196
  87.6 3.9 %copy-start.2 = (f32[4000]{0:T(1024)S(1)}, f32[4000]{0:T(1024)}, u32[]{:S(2)}) copy-start(f32[4000]{0:T(1024)} %param.17) | copy-start | bytes 48004
  91.3 60.3 %copy-start.3 = (f32[8,160,160]{2,1,0:T(8,128)S(1)}, f32[8,160,160]{2,1,0:T(8,128)}, u32[]{:S(2)}) copy-start(f32[8,160,160]{2,1,0:T(8,128)} %param.12) | copy-start | bytes 2457604
  91.3 60.3 %copy-start.5 = (f32[8,160]{1,0:T(8,128)S(1)}, f32[8,160]{1,0:T(8,128)}, u32[]{:S(2)}) copy-start(f32[8,160]{1,0:T(8,128)} %param.16) | copy-start | bytes 15364
  91.3 103.7 %all-gather.5.cloned.1.call-start = ((), (), s32[]{:S(2)}) async-start(), calls=%async_computation.2 | async-start | bytes 5898240 | tf_op jit(solution)/shard_map/all_gather | solution.py:38
  154.3 137.8 %all-reduce.5.cloned.1.call-start = ((), (), s32[]{:S(2)}) async-start(), calls=%async_computation.3 | async-start | bytes 2621440 | tf_op jit(solution)/shard_map/psum | solution.py:49
  206.9 22.4 %copy-start.4 = (f32[8,160,160]{2,1,0:T(8,128)S(1)}, f32[8,160,160]{2,1,0:T(8,128)}, u32[]{:S(2)}) copy-start(f32[8,160,160]{2,1,0:T(8,128)} %get-tuple-element.9) | copy-start | bytes 2457604
  292.1 3.4 %copy-start.1 = (bf16[8,160,768]{2,1,0:T(8,128)(2,1)S(1)}, bf16[8,160,768]{2,1,0:T(8,128)(2,1)}, u32[]{:S(2)}) copy-start(bf16[8,160,768]{2,1,0:T(8,128)(2,1)} %param.10) | copy-start | bytes 5898244
Sparse Core Ops, SparseCore 0:
  10.6 43.6 all-gather.2
  91.4 60.0 all-reduce.2
  154.4 40.5 all-gather.4
  232.0 60.0 all-reduce.4
where the time goes:
time: 302 us
  waiting for transfers between devices  203 us (67%)
  matrix products  47.4 us (16%)
  local copies, waits for them, and re-layouts  25.2 us (8%)
  between operations  13.9 us (5%)
  other arithmetic  12 us (4%)
    psum x2, waiting for transfers between devices, shards(): reduced = lax.psum(partial_sum, 'fit')  119 us
    all_gather x2, waiting for transfers between devices, shards(): everything = lax.all_gather(rounded, 'pairs', axis=0, tiled=True)  84.2 us
    dot_general x2, matrix products, shards(): jnp.einsum('rpad,rpbd->rpab', left_product, margins, preferred_element_ty...  43.7 us
    gather x2, local copies, waits for them, and re-layouts, shards(): fetched = everything[flat_partners]  23.7 us
  transfers between devices with their start and end apart: 4, of which 4 were waited for; matrix products, arithmetic and copies ran while one was open for 0% of the time, Pallas kernels for 0%

commit v1 on v0

--- a/solution.py
+++ b/solution.py
@@ -1,9 +1,24 @@
+import functools
 import jax
 import jax.numpy as jnp
 from jax import lax
 from jax.sharding import PartitionSpec as P
 
 ITERS = 2
+
+
+def _test_tokens(target, mesh_dim):
+    n = lax.psum(1, axis_name=mesh_dim)
+    t_next, then = (target, 0)
+    while 1 << then < n:
+        spare = tuple(((to_i, to_i ^ 1 << then) for to_i in range(n)))
+        r1 = lax.ppermute(t_next, axis_name=mesh_dim, perm=spare)
+        t_next = t_next + r1
+        then = then + 1
+    return t_next
+
+
+pair_routes_all = functools.partial(_test_tokens, mesh_dim="fit")
 
 
 def shards(
@@ -46,7 +61,7 @@
         )
         coupling = jnp.sum(fock_terms[:, :, None, None] * right_product, axis=1)
         partial_sum = integral_part - coupling
-        reduced = lax.psum(partial_sum, "fit")
+        reduced = pair_routes_all(partial_sum)
         residual = pair_mask * (reduced + denominator * amplitudes)
         amplitudes = amplitudes - residual / denominator
     return (amplitudes, residual)

time: 302 us -> 361 us (1.20)
  waiting for transfers between devices: 203 us -> 256 us
  starting transfers between devices: 0.34 us -> 8.11 us
    ppermute x0 -> x4, waiting for transfers between devices: none -> 171 us  [_test_tokens(): r1 = lax.ppermute(t_next, axis_name=mesh_dim, perm=spare)]
    psum x2 -> x0, waiting for transfers between devices: 119 us -> none  [shards(): reduced = lax.psum(partial_sum, 'fit')]
    ppermute x0 -> x4, starting transfers between devices: none -> 8.03 us  [_test_tokens(): r1 = lax.ppermute(t_next, axis_name=mesh_dim, perm=spare)]
  transfers between devices with their start and end apart: 4 -> 6, of which waited for: 4 -> 6; matrix products, arithmetic and copies ran while one was open for 0% -> 0% of each run, Pallas kernels for 0% -> 0%
where the time goes in v1:
time: 361 us
  waiting for transfers between devices  256 us (71%)
  matrix products  46.9 us (13%)
  local copies, waits for them, and re-layouts  25.2 us (7%)
  between operations  14.1 us (4%)
  other arithmetic  10.9 us (3%)
  starting transfers between devices  8.11 us (2%)
    ppermute x4, waiting for transfers between devices, _test_tokens(): r1 = lax.ppermute(t_next, axis_name=mesh_dim, perm=spare)  171 us
    all_gather x2, waiting for transfers between devices, shards(): everything = lax.all_gather(rounded, 'pairs', axis=0, tiled=True)  84.9 us
    dot_general x2, matrix products, shards(): jnp.einsum('rpad,rpbd->rpab', left_product, margins, preferred_element_ty...  43.6 us
    gather x2, local copies, waits for them, and re-layouts, shards(): fetched = everything[flat_partners]  23.8 us
    ppermute x4, starting transfers between devices, _test_tokens(): r1 = lax.ppermute(t_next, axis_name=mesh_dim, perm=spare)  8.03 us
  transfers between devices with their start and end apart: 6, of which 6 were waited for; matrix products, arithmetic and copies ran while one was open for 0% of the time, Pallas kernels for 0%

profile of v1, /device:TPU:0, one launch (start us, length us, event | category | flops | bytes accessed | tf_op | source)
XLA Modules:
  0.0 360.9 jit_solution(15766291592038929095)
XLA Ops:
  7.2 0.0 copy-start
  7.2 0.0 all-gather.3.cloned.1.call-start
  7.2 0.9 fusion.15
  8.1 0.0 copy-start.6
  8.1 2.4 fusion.14
  10.5 0.0 all-gather.3.cloned.1.call-update
  10.5 0.0 all-gather.5.cloned.1.call-start
  10.6 0.0 copy-done.6
  10.6 0.1 reshape.83
  10.7 0.0 copy-start.8
  10.7 43.7 %all-gather.3.cloned.1.call-done = bf16[64,160,160]{2,1,0:T(8,128)(2,1)} async-done(((bf16[8,160,160]{2,1,0:T(8,128)(2,1)}), bf16[64,160,160]{2,1,0:T(8,128)(2,1)}) %all-gather.3.cloned.1.call-update) | async-done | bytes 3276816 | tf_op jit(solution)/shard_map/all_gather | solution.py:53
  54.4 11.9 %gather_fusion = bf16[192,160,160]{2,1,0:T(8,128)(2,1)} fusion(bf16[64,160,160]{2,1,0:T(8,128)(2,1)} %all-gather.3.cloned.1.call-done, s32[1024]{0:T(1024)S(1)} %pad_clamp_fusion.2), kind=kCustom, calls=%fused_computation | custom fusion | bytes 19661568 | tf_op jit(solution)/shard_map/gather | solution.py:54
  66.3 0.0 copy-done.8
  66.3 21.3 %multiply_reduce_fusion.1 = f32[8,160,160]{2,1,0:T(8,128)S(1)} fusion(f32[8,24]{1,0:T(8,128)S(1)} %copy-done.8, bf16[8,24,160,160]{3,2,1,0:T(8,128)(2,1)} %param.13, bf16[8,24,160,160]{3,2,1,0:T(8,128)(2,1)} %bitcast.16), kind=kOutput, calls=%fused_computation.5 | convolution fusion | flops 3160268800 | bytes 20480768 | tf_op jit(solution)/shard_map/rpad,rpbd->rpab/dot_general | solution.py:59
  87.6 0.0 copy-done
  87.6 3.3 fusion.20
  90.9 0.0 copy-start.7
  90.9 0.0 copy-start.2
  90.9 0.0 copy-start.5
  90.9 1.5 collective-permute-start
  92.4 29.4 %collective-permute-done = f32[8,160,160]{2,1,0:T(8,128)S(1)} collective-permute-done((f32[8,160,160]{2,1,0:T(8,128)S(1)}, f32[8,160,160]{2,1,0:T(8,128)S(1)}, u32[]{:S(2)}, u32[]{:S(2)}) %collective-permute-start) | collective-permute-done | bytes 819232 | tf_op jit(solution)/shard_map/ppermute | solution.py:15
  121.8 0.0 copy-start.3
  121.8 0.2 add.58
  122.0 0.0 copy-start.4
  122.0 2.5 collective-permute-start.1
  124.5 0.0 copy-done.7
  124.5 0.0 copy-done.2
  124.6 0.6 gather_fusion.2
  125.2 0.6 gather_fusion.1
  125.8 0.0 copy-done.4
  125.9 55.4 %collective-permute-done.1 = f32[8,160,160]{2,1,0:T(8,128)} collective-permute-done((f32[8,160,160]{2,1,0:T(8,128)S(1)}, f32[8,160,160]{2,1,0:T(8,128)}, u32[]{:S(2)}, u32[]{:S(2)}) %collective-permute-start.1) | collective-permute-done | bytes 819232 | tf_op jit(solution)/shard_map/ppermute | solution.py:15
  181.2 0.0 copy-done.5
  181.2 0.0 copy-done.3
  181.2 3.2 fusion.18
  184.4 0.0 all-gather.5.cloned.1.call-update
  184.4 41.2 %all-gather.5.cloned.1.call-done = bf16[64,160,160]{2,1,0:T(8,128)(2,1)} async-done(((bf16[8,160,160]{2,1,0:T(8,128)(2,1)}), bf16[64,160,160]{2,1,0:T(8,128)(2,1)}) %all-gather.5.cloned.1.call-update) | async-done | bytes 3276816 | tf_op jit(solution)/shard_map/all_gather | solution.py:53
  225.6 11.9 %gather_fusion.3 = bf16[192,160,160]{2,1,0:T(8,128)(2,1)} fusion(bf16[64,160,160]{2,1,0:T(8,128)(2,1)} %all-gather.5.cloned.1.call-done, s32[1024]{0:T(1024)S(1)} %pad_clamp_fusion.2), kind=kCustom, calls=%fused_computation.3 | custom fusion | bytes 19661568 | tf_op jit(solution)/shard_map/gather | solution.py:54
  237.5 22.3 %multiply_reduce_fusion = f32[8,160,160]{2,1,0:T(8,128)} fusion(f32[8,24]{1,0:T(8,128)S(1)} %copy-done.8, bf16[8,24,160,160]{3,2,1,0:T(8,128)(2,1)} %param.13, bf16[8,24,160,160]{3,2,1,0:T(8,128)(2,1)} %bitcast.15), kind=kOutput, calls=%fused_computation.4 | convolution fusion | flops 3160268800 | bytes 20480768 | tf_op jit(solution)/shard_map/rpad,rpbd->rpab/dot_general | solution.py:59
  259.8 1.9 sub.24
  261.7 1.6 collective-permute-start.2
  263.3 29.4 %collective-permute-done.2 = f32[8,160,160]{2,1,0:T(8,128)S(1)} collective-permute-done((f32[8,160,160]{2,1,0:T(8,128)S(1)}, f32[8,160,160]{2,1,0:T(8,128)S(1)}, u32[]{:S(2)}, u32[]{:S(2)}) %collective-permute-start.2) | collective-permute-done | bytes 819232 | tf_op jit(solution)/shard_map/ppermute | solution.py:15
  292.7 0.2 add.67
  292.9 2.5 collective-permute-start.3
  295.4 56.6 %collective-permute-done.3 = f32[8,160,160]{2,1,0:T(8,128)S(1)} collective-permute-done((f32[8,160,160]{2,1,0:T(8,128)S(1)}, f32[8,160,160]{2,1,0:T(8,128)S(1)}, u32[]{:S(2)}, u32[]{:S(2)}) %collective-permute-start.3) | collective-permute-done | bytes 819232 | tf_op jit(solution)/shard_map/ppermute | solution.py:15
  352.0 0.0 copy-start.1
  352.0 2.1 divide_subtract_fusion
  354.1 0.0 copy-done.1
  (5 shorter events, 0.0 us)
Async XLA Ops:
  7.2 80.4 %copy-start = (bf16[8,160,768]{2,1,0:T(8,128)(2,1)S(1)}, bf16[8,160,768]{2,1,0:T(8,128)(2,1)}, u32[]{:S(2)}) copy-start(bf16[8,160,768]{2,1,0:T(8,128)(2,1)} %param.10) | copy-start | bytes 5898244
  7.2 47.2 %all-gather.3.cloned.1.call-start = ((), (), s32[]{:S(2)}) async-start(), calls=%async_computation | async-start | bytes 5898240 | tf_op jit(solution)/shard_map/all_gather | solution.py:53
  8.1 2.5 copy-start.6
  10.5 215.1 %all-gather.5.cloned.1.call-start = ((), (), s32[]{:S(2)}) async-start(), calls=%async_computation.1 | async-start | bytes 5898240 | tf_op jit(solution)/shard_map/all_gather | solution.py:53
  10.7 55.6 %copy-start.8 = (f32[8,24]{1,0:T(8,128)S(1)}, f32[8,24]{1,0:T(8,128)}, u32[]{:S(2)}) copy-start(f32[8,24]{1,0:T(8,128)} %param.14) | copy-start | bytes 2308
  90.9 33.7 %copy-start.7 = (s32[8,2]{0,1:T(2,128)S(1)}, s32[8,2]{0,1:T(2,128)}, u32[]{:S(2)}) copy-start(s32[8,2]{0,1:T(2,128)} %param.18) | copy-start | bytes 196
  90.9 33.7 %copy-start.2 = (f32[4000]{0:T(1024)S(1)}, f32[4000]{0:T(1024)}, u32[]{:S(2)}) copy-start(f32[4000]{0:T(1024)} %param.17) | copy-start | bytes 48004
  90.9 90.4 %copy-start.5 = (f32[8,160]{1,0:T(8,128)S(1)}, f32[8,160]{1,0:T(8,128)}, u32[]{:S(2)}) copy-start(f32[8,160]{1,0:T(8,128)} %param.16) | copy-start | bytes 15364
  90.9 30.9 %collective-permute-start = (f32[8,160,160]{2,1,0:T(8,128)S(1)}, f32[8,160,160]{2,1,0:T(8,128)S(1)}, u32[]{:S(2)}, u32[]{:S(2)}) collective-permute-start(f32[8,160,160]{2,1,0:T(8,128)S(1)} %get-tuple-element.8), channel_id=1, source_target_pairs={{0,1},{1,0},{2,3},{3,2},{4,5},{5,4},{6,7},{7,6},{8,9},{9,8},{10,11... | collective-permute-start | bytes 2457608 | tf_op jit(solution)/shard_map/ppermute | solution.py:15
  121.8 59.5 %copy-start.3 = (f32[8,160,160]{2,1,0:T(8,128)S(1)}, f32[8,160,160]{2,1,0:T(8,128)}, u32[]{:S(2)}) copy-start(f32[8,160,160]{2,1,0:T(8,128)} %param.12) | copy-start | bytes 2457604
  122.0 3.8 %copy-start.4 = (f32[8,160,160]{2,1,0:T(8,128)}, f32[8,160,160]{2,1,0:T(8,128)S(1)}, u32[]{:S(2)}) copy-start(f32[8,160,160]{2,1,0:T(8,128)S(1)} %add.58) | copy-start | bytes 2457604
  122.0 59.2 %collective-permute-start.1 = (f32[8,160,160]{2,1,0:T(8,128)S(1)}, f32[8,160,160]{2,1,0:T(8,128)}, u32[]{:S(2)}, u32[]{:S(2)}) collective-permute-start(f32[8,160,160]{2,1,0:T(8,128)S(1)} %add.58), channel_id=1, source_target_pairs={{0,2},{1,3},{2,0},{3,1},{4,6},{5,7},{6,4},{7,5},{8,10},{9,11},{10,... | collective-permute-start | bytes 2457608 | tf_op jit(solution)/shard_map/ppermute | solution.py:15
  261.7 31.0 %collective-permute-start.2 = (f32[8,160,160]{2,1,0:T(8,128)S(1)}, f32[8,160,160]{2,1,0:T(8,128)S(1)}, u32[]{:S(2)}, u32[]{:S(2)}) collective-permute-start(f32[8,160,160]{2,1,0:T(8,128)S(1)} %sub.24), channel_id=1, source_target_pairs={{0,1},{1,0},{2,3},{3,2},{4,5},{5,4},{6,7},{7,6},{8,9},{9,8},{10,11... | collective-permute-start | bytes 2457608 | tf_op jit(solution)/shard_map/ppermute | solution.py:15
  292.9 59.1 %collective-permute-start.3 = (f32[8,160,160]{2,1,0:T(8,128)S(1)}, f32[8,160,160]{2,1,0:T(8,128)S(1)}, u32[]{:S(2)}, u32[]{:S(2)}) collective-permute-start(f32[8,160,160]{2,1,0:T(8,128)S(1)} %add.67), channel_id=1, source_target_pairs={{0,2},{1,3},{2,0},{3,1},{4,6},{5,7},{6,4},{7,5},{8,10},{9,11},{10,... | collective-permute-start | bytes 2457608 | tf_op jit(solution)/shard_map/ppermute | solution.py:15
  352.0 2.1 copy-start.1
Sparse Core Ops, SparseCore 0:
  10.6 43.6 all-gather.2
  184.6 40.9 all-gather.4
